TPU v7x, 32 devices: a whole 2x2x4 slice. The times are simulated.
32 devices in a mesh: ctx: 4 (over y, x), grp: 4 (over z), side: 2 (over core).
Axes of the slice: x: 2, y: 2, z: 4, core: 2. Of those that a mesh axis runs over, the one named last changes fastest.
Arguments:
- tokens: bfloat16 [512, 2048], P(('ctx', 'grp', 'side')), may hold values from -6 to 6
- norm_gain: float32 [2048], replicated, may hold values from 0.25 to 1.75
- combine: float32 [512, 8], P(('ctx', 'grp', 'side')), may hold values from 0.05 to 0.6
- expert_ids: int32 [512, 8], P(('ctx', 'grp', 'side')), may hold values from 0 to 15, all different within a row; in each aligned block of 16 rows (0 to 15, 16 to 31, ...) at most 11 rows name the same one
- w_gate: bfloat16 [16, 2048, 768], P(('ctx', 'grp'), None, 'side'), may hold values from -0.125 to 0.125
- w_up: bfloat16 [16, 2048, 768], P(('ctx', 'grp'), None, 'side'), may hold values from -0.125 to 0.125
- w_down: bfloat16 [16, 768, 2048], P(('ctx', 'grp'), 'side'), may hold values from -0.21875 to 0.21875
- d_out: bfloat16 [512, 2048], P(('ctx', 'grp', 'side')), may hold values from -6 to 6
Outputs:
- mixed: bfloat16 [512, 2048], P(('ctx', 'grp', 'side'))
- d_tokens: bfloat16 [512, 2048], P(('ctx', 'grp', 'side'))
- d_gain: float32 [2048], replicated
- d_combine: float32 [512, 8], P(('ctx', 'grp', 'side'))
- d_w_gate: bfloat16 [16, 2048, 768], P(('ctx', 'grp'), None, 'side')
- d_w_up: bfloat16 [16, 2048, 768], P(('ctx', 'grp'), None, 'side')
- d_w_down: bfloat16 [16, 768, 2048], P(('ctx', 'grp'), 'side')
Inputs may be any that keep to these rules, and one draw needn't show every extreme that they name: `expert_ids`: each row names 8 different experts; among the 16 rows of one device no expert is named more than 11 times, and that bound is reached.
All inputs are finite; a program needn't handle non-finite values.
Results may differ from a plain program's by a relative error of at most 0.0072.
Values may be sent and summed in bfloat16 or wider, within the bound.
A program may use at most 128 MiB of HBM per device.

v0:
```python
import jax
import jax.numpy as jnp
from jax import lax
from jax.sharding import PartitionSpec as P

EPS = 1e-06


def expert_pass(rows, grads, gate_w, up_w, down_w):
    a_gate = jnp.dot(rows, gate_w, preferred_element_type=jnp.float32)
    a_up = jnp.dot(rows, up_w, preferred_element_type=jnp.float32)
    sigmoid_gate = jax.nn.sigmoid(a_gate)
    silu_gate = a_gate * sigmoid_gate
    hidden = (silu_gate * a_up).astype(jnp.bfloat16)
    output = jnp.dot(hidden, down_w, preferred_element_type=jnp.float32)
    d_hidden = lax.dot_general(
        grads, down_w, (((1,), (1,)), ((), ())), preferred_element_type=jnp.float32
    )
    d_up = (d_hidden * silu_gate).astype(jnp.bfloat16)
    d_gate = (d_hidden * a_up * sigmoid_gate * (1.0 + a_gate * (1.0 - sigmoid_gate))).astype(
        jnp.bfloat16
    )
    d_rows = lax.dot_general(
        d_gate, gate_w, (((1,), (1,)), ((), ())), preferred_element_type=jnp.float32
    )
    d_rows = d_rows + lax.dot_general(
        d_up, up_w, (((1,), (1,)), ((), ())), preferred_element_type=jnp.float32
    )
    g_gate = lax.dot_general(
        rows, d_gate, (((0,), (0,)), ((), ())), preferred_element_type=jnp.float32
    )
    g_up = lax.dot_general(rows, d_up, (((0,), (0,)), ((), ())), preferred_element_type=jnp.float32)
    g_down = lax.dot_general(
        hidden, grads, (((0,), (0,)), ((), ())), preferred_element_type=jnp.float32
    )
    return (output, d_rows, g_gate, g_up, g_down)


def local(tokens, norm_gain, combine, expert_ids, w_gate, w_up, w_down, d_out):
    count = tokens.shape[0]
    width = tokens.shape[1]
    chosen = expert_ids.shape[1]
    n_ctx = lax.axis_size("ctx")
    n_grp = lax.axis_size("grp")
    experts = n_ctx * n_grp
    slots = max(2, (4 * count * chosen + 3 * experts - 1) // (3 * experts))
    places = experts * slots
    x_float = tokens.astype(jnp.float32)
    inv_rms = lax.rsqrt(jnp.mean(x_float * x_float, axis=1, keepdims=True) + EPS)
    normed = (x_float * inv_rms * norm_gain).astype(jnp.bfloat16)
    grad_float = d_out.astype(jnp.float32)
    flat_ids = expert_ids.reshape(-1)
    onehot = (flat_ids[:, None] == jnp.arange(experts, dtype=jnp.int32)[None, :]).astype(jnp.int32)
    before = jnp.cumsum(onehot, axis=0) - onehot
    slot = jnp.sum(before * onehot, axis=1)
    target = flat_ids * slots + slot
    select = (target[:, None] == jnp.arange(places, dtype=jnp.int32)[None, :]).astype(jnp.float32)
    per_token = select.reshape(count, chosen, places)
    token_map = jnp.sum(per_token, axis=1).astype(jnp.bfloat16)
    weighted = jnp.sum(per_token * combine[:, :, None], axis=1)
    send_rows = lax.dot_general(
        token_map, normed, (((0,), (0,)), ((), ())), preferred_element_type=jnp.float32
    ).astype(jnp.bfloat16)
    send_grads = lax.dot_general(
        weighted,
        grad_float,
        (((0,), (0,)), ((), ())),
        precision=lax.Precision.HIGHEST,
        preferred_element_type=jnp.float32,
    ).astype(jnp.bfloat16)
    rows_in, grads_in = (
        lax.all_to_all(
            send_rows.reshape(experts, slots, width),
            ("ctx", "grp"),
            split_axis=0,
            concat_axis=0,
            tiled=True,
        ),
        lax.all_to_all(
            send_grads.reshape(experts, slots, width),
            ("ctx", "grp"),
            split_axis=0,
            concat_axis=0,
            tiled=True,
        ),
    )
    full_gate, full_up, full_down = (
        lax.all_gather(w_gate[0], "side", axis=1, tiled=True),
        lax.all_gather(w_up[0], "side", axis=1, tiled=True),
        lax.all_gather(w_down[0], "side", axis=0, tiled=True),
    )
    output, d_rows, g_gate, g_up, g_down = expert_pass(
        rows_in.reshape(places, width),
        grads_in.reshape(places, width),
        full_gate,
        full_up,
        full_down,
    )
    own_gate, own_up, own_down = (
        lax.psum_scatter(g_gate, "side", scatter_dimension=1, tiled=True),
        lax.psum_scatter(g_up, "side", scatter_dimension=1, tiled=True),
        lax.psum_scatter(g_down, "side", scatter_dimension=0, tiled=True),
    )
    back_out = output.astype(jnp.bfloat16)
    back_rows = d_rows.astype(jnp.bfloat16)
    came_out, came_rows = (
        lax.all_to_all(
            back_out.reshape(experts, slots, width),
            ("ctx", "grp"),
            split_axis=0,
            concat_axis=0,
            tiled=True,
        ),
        lax.all_to_all(
            back_rows.reshape(experts, slots, width),
            ("ctx", "grp"),
            split_axis=0,
            concat_axis=0,
            tiled=True,
        ),
    )
    slot_out = jnp.dot(
        select.astype(jnp.bfloat16),
        came_out.reshape(places, width),
        preferred_element_type=jnp.float32,
    ).reshape(count, chosen, width)
    mixed = (x_float + jnp.sum(combine[:, :, None] * slot_out, axis=1)).astype(jnp.bfloat16)
    d_combine = jnp.einsum("tkd,td->tk", slot_out, grad_float, precision=lax.Precision.HIGHEST)
    d_normed = jnp.dot(
        token_map, came_rows.reshape(places, width), preferred_element_type=jnp.float32
    )
    d_gain = lax.psum(jnp.sum(d_normed * x_float * inv_rms, axis=0), ("ctx", "grp", "side"))
    scaled = d_normed * norm_gain
    d_tokens = (
        grad_float
        + inv_rms * scaled
        - x_float * inv_rms**3 * jnp.mean(scaled * x_float, axis=1, keepdims=True)
    )
    return (
        mixed,
        d_tokens.astype(jnp.bfloat16),
        d_gain,
        d_combine,
        own_gate.astype(jnp.bfloat16)[None],
        own_up.astype(jnp.bfloat16)[None],
        own_down.astype(jnp.bfloat16)[None],
    )


def solution(mesh):
    in_specs = (
        P(("ctx", "grp", "side"), None),
        P(),
        P(("ctx", "grp", "side"), None),
        P(("ctx", "grp", "side"), None),
        P(("ctx", "grp"), None, "side"),
        P(("ctx", "grp"), None, "side"),
        P(("ctx", "grp"), "side", None),
        P(("ctx", "grp", "side"), None),
    )
    out_specs = (
        P(("ctx", "grp", "side"), None),
        P(("ctx", "grp", "side"), None),
        P(),
        P(("ctx", "grp", "side"), None),
        P(("ctx", "grp"), None, "side"),
        P(("ctx", "grp"), None, "side"),
        P(("ctx", "grp"), "side", None),
    )
    return jax.shard_map(local, mesh=mesh, in_specs=in_specs, out_specs=out_specs, check_vma=False)
```

profile of v0, /device:TPU:0, one launch (start us, length us, event | category | flops | bytes accessed | tf_op | source)
XLA Modules:
  0.0 221.6 jit_solution(12201147010498002594)
XLA Ops:
  7.2 0.7 all-gather.11.cloned.1.call-update
  8.0 0.7 all-gather.9.cloned.1.call-update
  9.7 0.8 convolution_convert_fusion
  10.5 1.2 reshape.111
  11.7 8.3 %all-to-all-start.2 = ((bf16[16,11,2048]{2,1,0:T(8,128)(2,1)}), bf16[16,11,2048]{2,1,0:T(8,128)(2,1)S(1)}, u32[]{:S(2)}, u32[]{:S(2)}) async-start(bf16[16,11,2048]{2,1,0:T(8,128)(2,1)} %reshape.111), calls=%async_computation.2 | async-start | bytes 2097152 | tf_op jit(solution)/shard_map/all_to_all | solution.py:79
  20.1 0.7 all-gather.7.cloned.1.call-update
  21.9 1.2 reshape.107
  23.1 24.4 %all-to-all-done.2 = bf16[16,11,2048]{2,1,0:T(8,128)(2,1)S(1)} async-done(((bf16[16,11,2048]{2,1,0:T(8,128)(2,1)}), bf16[16,11,2048]{2,1,0:T(8,128)(2,1)S(1)}, u32[]{:S(2)}, u32[]{:S(2)}) %all-to-all-start.2) | async-done | bytes 720928 | tf_op jit(solution)/shard_map/all_to_all | solution.py:79
  47.5 3.7 %all-to-all-start = ((bf16[16,11,2048]{2,1,0:T(8,128)(2,1)}), bf16[16,11,2048]{2,1,0:T(8,128)(2,1)S(1)}, u32[]{:S(2)}, u32[]{:S(2)}) async-start(bf16[16,11,2048]{2,1,0:T(8,128)(2,1)} %reshape.107), calls=%async_computation | async-start | bytes 2097152 | tf_op jit(solution)/shard_map/all_to_all | solution.py:72
  51.5 26.4 %all-to-all-done = bf16[16,11,2048]{2,1,0:T(8,128)(2,1)S(1)} async-done(((bf16[16,11,2048]{2,1,0:T(8,128)(2,1)}), bf16[16,11,2048]{2,1,0:T(8,128)(2,1)S(1)}, u32[]{:S(2)}, u32[]{:S(2)}) %all-to-all-start) | async-done | bytes 720928 | tf_op jit(solution)/shard_map/all_to_all | solution.py:72
  78.3 3.1 %fusion = f32[176,768]{1,0:T(8,128)S(1)} fusion(bf16[176,2048]{1,0:T(8,128)(2,1)S(1)} %reshape.112, bf16[1,768,2048]{2,1,0:T(8,128)(2,1)} %all-gather.11.cloned.1.call-done), kind=kOutput, calls=%fused_computation | convolution fusion | flops 553648128 | bytes 4407296 | tf_op jit(solution)/shard_map/dot_general | solution.py:16
  81.4 2.6 %fusion.6 = f32[176,768]{1,0:T(8,128)S(1)} fusion(bf16[176,2048]{1,0:T(8,128)(2,1)S(1)} %reshape.108, bf16[1,2048,768]{2,1,0:T(8,128)(2,1)} %all-gather.9.cloned.1.call-done), kind=kOutput, calls=%fused_computation.6 | convolution fusion | flops 553648128 | bytes 4407296 | tf_op jit(solution)/shard_map/dot_general | solution.py:11
  84.1 2.8 %multiply_convert_fusion.1 = (bf16[176,768]{1,0:T(8,128)(2,1)S(1)}, bf16[176,768]{1,0:T(8,128)(2,1)S(1)}, bf16[176,768]{1,0:T(8,128)(2,1)S(1)}) fusion(f32[176,768]{1,0:T(8,128)S(1)} %fusion, f32[176,768]{1,0:T(8,128)S(1)} %fusion.6, bf16[176,2048]{1,0:T(8,128)(2,1)S(1)} %reshape.108, bf16[1,2048,768]{2,1,0:T(8,128)(2,1)} %all-gather.7.cloned.1.call-done), kind=kOutput, calls=%fused_computation.22 | convolution fusion | flops 555675648 | bytes 5758976 | tf_op jit(solution)/shard_map/dot_general | solution.py:10
  86.9 3.6 %fusion.47 = f32[768,2048]{1,0:T(8,128)} fusion(bf16[176,768]{1,0:T(8,128)(2,1)S(1)} %get-tuple-element.13, bf16[176,2048]{1,0:T(8,128)(2,1)S(1)} %reshape.112), kind=kOutput, calls=%fused_computation.66 | convolution fusion | flops 553648128 | bytes 7282688 | tf_op jit(solution)/shard_map/dot_general | solution.py:33
  90.6 4.0 %fusion.45 = f32[2048,768]{1,0:T(8,128)} fusion(bf16[176,2048]{1,0:T(8,128)(2,1)S(1)} %reshape.108, bf16[176,768]{1,0:T(8,128)(2,1)S(1)} %get-tuple-element.11), kind=kOutput, calls=%fused_computation.64 | convolution fusion | flops 553648128 | bytes 7282688 | tf_op jit(solution)/shard_map/dot_general | solution.py:29
  94.7 4.8 %fusion.46 = f32[2048,768]{1,0:T(8,128)} fusion(bf16[176,2048]{1,0:T(8,128)(2,1)S(1)} %reshape.108, bf16[176,768]{1,0:T(8,128)(2,1)S(1)} %get-tuple-element.12), kind=kOutput, calls=%fused_computation.65 | convolution fusion | flops 553648128 | bytes 7282688 | tf_op jit(solution)/shard_map/dot_general | solution.py:32
  99.5 3.9 %fusion.15 = bf16[176,2048]{1,0:T(8,128)(2,1)} fusion(bf16[176,768]{1,0:T(8,128)(2,1)S(1)} %get-tuple-element.13, bf16[1,768,2048]{2,1,0:T(8,128)(2,1)} %all-gather.11.cloned.1.call-done), kind=kOutput, calls=%fused_computation.13 | convolution fusion | flops 554008576 | bytes 4136960 | tf_op jit(solution)/shard_map/dot_general | solution.py:15
  103.4 2.3 %reshape.109 = bf16[16,11,2048]{2,1,0:T(8,128)(2,1)} reshape(bf16[176,2048]{1,0:T(8,128)(2,1)} %fusion.15) | data formatting | bytes 1441792 | tf_op jit(solution)/shard_map/reshape | solution.py:108
  105.7 4.5 %all-to-all-start.1 = ((bf16[16,11,2048]{2,1,0:T(8,128)(2,1)}), bf16[16,11,2048]{2,1,0:T(8,128)(2,1)}, u32[]{:S(2)}, u32[]{:S(2)}) async-start(bf16[16,11,2048]{2,1,0:T(8,128)(2,1)} %reshape.109), calls=%async_computation.1 | async-start | bytes 2097152 | tf_op jit(solution)/shard_map/all_to_all | solution.py:107
  110.2 2.3 %fusion.4 = f32[176,2048]{1,0:T(8,128)S(1)} fusion(bf16[176,768]{1,0:T(8,128)(2,1)} %copy-done.4, bf16[1,2048,768]{2,1,0:T(8,128)(2,1)S(1)} %copy-done), kind=kOutput, calls=%fused_computation.4 | convolution fusion | flops 553648128 | bytes 4857856 | tf_op jit(solution)/shard_map/dot_general | solution.py:26
  112.5 1.2 fusion.18
  113.7 1.2 reshape.113
  115.0 21.5 %all-to-all-done.1 = bf16[16,11,2048]{2,1,0:T(8,128)(2,1)} async-done(((bf16[16,11,2048]{2,1,0:T(8,128)(2,1)}), bf16[16,11,2048]{2,1,0:T(8,128)(2,1)}, u32[]{:S(2)}, u32[]{:S(2)}) %all-to-all-start.1) | async-done | bytes 720928 | tf_op jit(solution)/shard_map/all_to_all | solution.py:107
  136.5 3.8 %all-to-all-start.3 = ((bf16[16,11,2048]{2,1,0:T(8,128)(2,1)}), bf16[16,11,2048]{2,1,0:T(8,128)(2,1)S(1)}, u32[]{:S(2)}, u32[]{:S(2)}) async-start(bf16[16,11,2048]{2,1,0:T(8,128)(2,1)} %reshape.113), calls=%async_computation.3 | async-start | bytes 2097152 | tf_op jit(solution)/shard_map/all_to_all | solution.py:114
  140.3 1.5 reshape.118
  142.4 1.1 fusion.32
  144.2 22.6 %all-to-all-done.3 = bf16[16,11,2048]{2,1,0:T(8,128)(2,1)S(1)} async-done(((bf16[16,11,2048]{2,1,0:T(8,128)(2,1)}), bf16[16,11,2048]{2,1,0:T(8,128)(2,1)S(1)}, u32[]{:S(2)}, u32[]{:S(2)}) %all-to-all-start.3) | async-done | bytes 720928 | tf_op jit(solution)/shard_map/all_to_all | solution.py:114
  167.5 36.9 %psum.7 = f32[2048]{0:T(1024)} all-reduce(f32[2048]{0:T(1024)S(1)} %get-tuple-element.7), channel_id=1, replica_groups=mesh['ctx'=4,'grp'=4,'side'=2] {'ctx','grp','side'}, use_global_device_ids=true, to_apply=%region_8.9 | all-reduce | flops 2048 | bytes 16384 | tf_op jit(solution)/shard_map/psum | solution.py:132
  204.4 0.7 fusion.28
  205.1 3.3 %convert_bitcast_fusion = bf16[1,384,2048]{2,1,0:T(8,128)(2,1)} fusion(f32[384,2048]{1,0:T(8,128)} %reduce-scatter.8.cloned.1.call-done), kind=kLoop, calls=%fused_computation.17 | loop fusion | flops 786432 | bytes 4718592 | tf_op jit(solution)/shard_map/broadcast_in_dim | solution.py:146
  208.4 3.2 %convert_bitcast_fusion.2 = bf16[1,2048,384]{2,1,0:T(8,128)(2,1)} fusion(f32[2048,384]{1,0:T(8,128)} %reduce-scatter.4.cloned.1.call-done), kind=kLoop, calls=%fused_computation.19 | loop fusion | flops 786432 | bytes 4718592 | tf_op jit(solution)/shard_map/broadcast_in_dim | solution.py:144
  211.6 3.2 %convert_bitcast_fusion.1 = bf16[1,2048,384]{2,1,0:T(8,128)(2,1)} fusion(f32[2048,384]{1,0:T(8,128)} %reduce-scatter.6.cloned.1.call-done), kind=kLoop, calls=%fused_computation.18 | loop fusion | flops 786432 | bytes 4718592 | tf_op jit(solution)/shard_map/broadcast_in_dim | solution.py:145
  (72 shorter events, 4.7 us)
Async XLA Ops:
  7.2 1.5 copy-start.16
  7.2 1.6 copy-start.17
  7.2 2.5 %copy-start.5 = (bf16[16,2048]{1,0:T(8,128)(2,1)S(1)}, bf16[16,2048]{1,0:T(8,128)(2,1)}, u32[]{:S(2)}) copy-start(bf16[16,2048]{1,0:T(8,128)(2,1)} %param.15) | copy-start | bytes 196612
  7.2 71.1 %all-gather.11.cloned.1.call-start = ((), (), s32[]{:S(2)}) async-start(), calls=%async_computation.12 | async-start | bytes 4718592 | tf_op jit(solution)/shard_map/all_gather | solution.py:90
  7.9 73.5 %all-gather.9.cloned.1.call-start = ((), (), s32[]{:S(2)}) async-start(), calls=%async_computation.11 | async-start | bytes 4718592 | tf_op jit(solution)/shard_map/all_gather | solution.py:89
  8.8 12.0 %copy-start.12 = (f32[16,8]{1,0:T(8,128)}, f32[16,8]{1,0:T(8,128)S(1)}, u32[]{:S(2)}) copy-start(f32[16,8]{1,0:T(8,128)S(1)} %copy.23) | copy-start | bytes 1540
  9.5 11.5 %copy-start.10 = (s32[16,8]{1,0:T(8,128)}, s32[16,8]{1,0:T(8,128)S(1)}, u32[]{:S(2)}) copy-start(s32[16,8]{1,0:T(8,128)S(1)} %multiply_add_fusion) | copy-start | bytes 1540
  9.5 11.3 %copy-start.6 = (bf16[16,2048]{1,0:T(8,128)(2,1)S(1)}, bf16[16,2048]{1,0:T(8,128)(2,1)}, u32[]{:S(2)}) copy-start(bf16[16,2048]{1,0:T(8,128)(2,1)} %param.8) | copy-start | bytes 196612
  9.7 11.8 %copy-start.8 = (bf16[16,176]{1,0:T(8,128)(2,1)}, bf16[16,176]{1,0:T(8,128)(2,1)S(1)}, u32[]{:S(2)}) copy-start(bf16[16,176]{1,0:T(8,128)(2,1)S(1)} %get-tuple-element.10) | copy-start | bytes 16900
  9.7 11.8 %copy-start.7 = (f32[2048]{0:T(1024)S(1)}, f32[2048]{0:T(1024)}, u32[]{:S(2)}) copy-start(f32[2048]{0:T(1024)} %param.9) | copy-start | bytes 24580
  11.7 35.8 %all-to-all-start.2 = ((bf16[16,11,2048]{2,1,0:T(8,128)(2,1)}), bf16[16,11,2048]{2,1,0:T(8,128)(2,1)S(1)}, u32[]{:S(2)}, u32[]{:S(2)}) async-start(bf16[16,11,2048]{2,1,0:T(8,128)(2,1)} %reshape.111), calls=%async_computation.2 | async-start | bytes 2097152 | tf_op jit(solution)/shard_map/all_to_all | solution.py:79
  20.0 64.0 %all-gather.7.cloned.1.call-start = ((), (), s32[]{:S(2)}) async-start(), calls=%async_computation.10 | async-start | bytes 4718592 | tf_op jit(solution)/shard_map/all_gather | solution.py:88
  21.5 26.0 %copy-start.14 = (f32[16]{0:T(128)}, f32[16]{0:T(128)S(1)}, u32[]{:S(2)}) copy-start(f32[16]{0:T(128)S(1)} %get-tuple-element.17) | copy-start | bytes 196
  47.5 30.5 %all-to-all-start = ((bf16[16,11,2048]{2,1,0:T(8,128)(2,1)}), bf16[16,11,2048]{2,1,0:T(8,128)(2,1)S(1)}, u32[]{:S(2)}, u32[]{:S(2)}) async-start(bf16[16,11,2048]{2,1,0:T(8,128)(2,1)} %reshape.107), calls=%async_computation | async-start | bytes 2097152 | tf_op jit(solution)/shard_map/all_to_all | solution.py:72
  51.2 153.9 %reduce-scatter.8.cloned.1.call-start = ((), (), s32[]{:S(2)}) async-start(), calls=%async_computation.9 | async-start | bytes 9437184 | tf_op jit(solution)/shard_map/reduce_scatter | solution.py:102
  86.9 3.7 %copy-start.2 = (bf16[176,768]{1,0:T(8,128)(2,1)}, bf16[176,768]{1,0:T(8,128)(2,1)S(1)}, u32[]{:S(2)}) copy-start(bf16[176,768]{1,0:T(8,128)(2,1)S(1)} %get-tuple-element.11) | copy-start | bytes 811012
  86.9 7.8 %copy-start.4 = (bf16[176,768]{1,0:T(8,128)(2,1)}, bf16[176,768]{1,0:T(8,128)(2,1)S(1)}, u32[]{:S(2)}) copy-start(bf16[176,768]{1,0:T(8,128)(2,1)S(1)} %get-tuple-element.12) | copy-start | bytes 811012
  90.5 117.8 %reduce-scatter.4.cloned.1.call-start = ((), (), s32[]{:S(2)}) async-start(), calls=%async_computation.7 | async-start | bytes 9437184 | tf_op jit(solution)/shard_map/reduce_scatter | solution.py:100
  94.6 116.9 %reduce-scatter.6.cloned.1.call-start = ((), (), s32[]{:S(2)}) async-start(), calls=%async_computation.8 | async-start | bytes 9437184 | tf_op jit(solution)/shard_map/reduce_scatter | solution.py:101
  99.5 10.7 %copy-start = (bf16[1,2048,768]{2,1,0:T(8,128)(2,1)S(1)}, bf16[1,2048,768]{2,1,0:T(8,128)(2,1)}, u32[]{:S(2)}) copy-start(bf16[1,2048,768]{2,1,0:T(8,128)(2,1)} %all-gather.9.cloned.1.call-done) | copy-start | bytes 9437188
  105.7 6.8 %copy-start.3 = (bf16[176,768]{1,0:T(8,128)(2,1)S(1)}, bf16[176,768]{1,0:T(8,128)(2,1)}, u32[]{:S(2)}) copy-start(bf16[176,768]{1,0:T(8,128)(2,1)} %copy-done.2) | copy-start | bytes 811012
  105.7 30.7 %all-to-all-start.1 = ((bf16[16,11,2048]{2,1,0:T(8,128)(2,1)}), bf16[16,11,2048]{2,1,0:T(8,128)(2,1)}, u32[]{:S(2)}, u32[]{:S(2)}) async-start(bf16[16,11,2048]{2,1,0:T(8,128)(2,1)} %reshape.109), calls=%async_computation.1 | async-start | bytes 2097152 | tf_op jit(solution)/shard_map/all_to_all | solution.py:107
  110.2 2.3 %copy-start.1 = (bf16[1,2048,768]{2,1,0:T(8,128)(2,1)S(1)}, bf16[1,2048,768]{2,1,0:T(8,128)(2,1)}, u32[]{:S(2)}) copy-start(bf16[1,2048,768]{2,1,0:T(8,128)(2,1)} %all-gather.7.cloned.1.call-done) | copy-start | bytes 9437188
  113.7 28.1 %copy-start.11 = (s32[16,8]{1,0:T(8,128)S(1)}, s32[16,8]{1,0:T(8,128)}, u32[]{:S(2)}) copy-start(s32[16,8]{1,0:T(8,128)} %copy-done.10) | copy-start | bytes 1540
  113.7 28.1 %copy-start.13 = (f32[16,8]{1,0:T(8,128)S(1)}, f32[16,8]{1,0:T(8,128)}, u32[]{:S(2)}) copy-start(f32[16,8]{1,0:T(8,128)} %copy-done.12) | copy-start | bytes 1540
  136.5 30.4 %all-to-all-start.3 = ((bf16[16,11,2048]{2,1,0:T(8,128)(2,1)}), bf16[16,11,2048]{2,1,0:T(8,128)(2,1)S(1)}, u32[]{:S(2)}, u32[]{:S(2)}) async-start(bf16[16,11,2048]{2,1,0:T(8,128)(2,1)} %reshape.113), calls=%async_computation.3 | async-start | bytes 2097152 | tf_op jit(solution)/shard_map/all_to_all | solution.py:114
  140.3 26.8 %copy-start.9 = (bf16[16,176]{1,0:T(8,128)(2,1)S(1)}, bf16[16,176]{1,0:T(8,128)(2,1)}, u32[]{:S(2)}) copy-start(bf16[16,176]{1,0:T(8,128)(2,1)} %copy-done.8) | copy-start | bytes 16900
  140.3 26.8 %copy-start.15 = (f32[16]{0:T(128)S(1)}, f32[16]{0:T(128)}, u32[]{:S(2)}) copy-start(f32[16]{0:T(128)} %copy-done.14) | copy-start | bytes 196
  141.9 62.5 %copy-start.18 = (f32[16]{0:T(128)S(1)}, f32[16]{0:T(128)}, u32[]{:S(2)}) copy-start(f32[16]{0:T(128)} %get-tuple-element.16) | copy-start | bytes 196
Sparse Core Ops, SparseCore 0:
  9.6 14.8 all-gather.10
  26.0 13.1 all-gather.8
  40.8 13.1 all-gather.6
  90.6 11.2 reduce-scatter.7
  104.1 15.8 reduce-scatter.3
  122.1 15.0 reduce-scatter.5
where the time goes:
time: 223 us; the launch traced here: 222 us
  waiting for transfers between devices  97.2 us (44%)
  blocking collectives  36.9 us (17%)
  matrix products  31.3 us (14%)
  starting transfers between devices  20.6 us (9%)
  between operations  14.5 us (7%)
  other arithmetic  11.7 us (5%)
  local copies, waits for them, and re-layouts  9.45 us (4%)
    psum x1, blocking collectives, local(): lax.psum(jnp.sum(d_normed * x_float * inv_rms, axis=0), ('ctx', 'grp', 's...  36.9 us
    all_to_all x1, waiting for transfers between devices, local(): lax.all_to_all(send_rows.reshape(experts, slots, width), ('ctx', 'grp'),...  26.4 us
    all_to_all x1, waiting for transfers between devices, local(): lax.all_to_all(send_grads.reshape(experts, slots, width), ('ctx', 'grp'),...  24.4 us
    all_to_all x1, waiting for transfers between devices, local(): lax.all_to_all(back_rows.reshape(experts, slots, width), ('ctx', 'grp'),...  22.6 us
    all_to_all x1, waiting for transfers between devices, local(): lax.all_to_all(back_out.reshape(experts, slots, width), ('ctx', 'grp'), s...  21.5 us
    all_to_all x1, starting transfers between devices, local(): lax.all_to_all(send_grads.reshape(experts, slots, width), ('ctx', 'grp'),...  8.34 us
    dot_general x1, matrix products, expert_pass(): lax.dot_general(rows, d_up, (((0,), (0,)), ((), ())), preferred_element_t...  4.81 us
    all_to_all x1, starting transfers between devices, local(): lax.all_to_all(back_out.reshape(experts, slots, width), ('ctx', 'grp'), s...  4.48 us
  transfers between devices with their start and end apart: 10, of which 4 were waited for; matrix products, arithmetic and copies ran while one was open for 19% of the time, Pallas kernels for 0%

commit v1 on v0

--- a/solution.py
+++ b/solution.py
@@ -1,6 +1,8 @@
 import jax
 import jax.numpy as jnp
 from jax import lax
+from jax.experimental import pallas as pl
+from jax.experimental.pallas import tpu as pltpu
 from jax.sharding import PartitionSpec as P
 
 EPS = 1e-06
@@ -147,6 +149,435 @@
     )
 
 
+MESH = pl.DeviceIdType.MESH
+LANES = 128
+
+
+def fits(mesh):
+    return mesh.shape["ctx"] == 4 and mesh.shape["side"] == 2 and mesh.shape["grp"] <= 4
+
+
+def kernel(
+    n_grp,
+    tok_ref, gain_ref, comb_ref, ids_ref, wg_hbm, wu_hbm, wd_hbm, dout_ref,
+    mixed_ref, dtok_ref, dgain_ref, dcomb_ref, gg_hbm, gu_hbm, gd_hbm,
+    xg, dg, wg, wu, wd, cw, mo, bo, rs, rp1, rp2, rz, dgb, act, gwg, gwu, gwd, acc,
+    zs_s, zs_r, p1_s, p1_r, p2_s, p2_r, sd_s, sd_r,
+    rs_s, rs_r, q1_s, q1_r, q2_s, q2_r, rz_s, rz_r, dg_s, dg_r, w_sem, o_sem,
+):
+    G = n_grp
+    count, width = tok_ref.shape
+    full = xg.shape[2]
+    half = wg.shape[1]
+    chunks = xg.shape[0]
+    total = chunks * count
+    c, g, s = lax.axis_index("ctx"), lax.axis_index("grp"), lax.axis_index("side")
+    x, y = c % 2, c // 2
+    cx, cy, cxy = y * 2 + (1 - x), (1 - y) * 2 + x, (1 - y) * 2 + (1 - x)
+    o = 1 - s
+    expert = c * G + g
+    bf, f32 = jnp.bfloat16, jnp.float32
+
+    def idx(cc, gg, ss):
+        return (cc * G + gg) * 2 + ss
+
+    def rc(src, dst, ssem, rsem, dev):
+        return pltpu.make_async_remote_copy(
+            src_ref=src, dst_ref=dst, send_sem=ssem, recv_sem=rsem, device_id=dev, device_id_type=MESH
+        )
+
+    loads = [
+        pltpu.make_async_copy(a.at[0], b, w_sem.at[i])
+        for i, (a, b) in enumerate(((wg_hbm, wg), (wu_hbm, wu), (wd_hbm, wd)))
+    ]
+
+    barrier = pltpu.get_barrier_semaphore()
+    peers = [(cx, g, s), (cy, g, s), (c, g, o)] + [(c, (g + k) % G, s) for k in range(1, G)]
+    for dev in peers:
+        pl.semaphore_signal(barrier, inc=1, device_id=dev, device_id_type=MESH)
+
+    x_f = tok_ref[...].astype(f32)
+    inv = lax.rsqrt(jnp.mean(x_f * x_f, axis=1, keepdims=True) + EPS)
+    lane = lax.broadcasted_iota(jnp.int32, (count, LANES), 1)
+    table = jnp.zeros((count, LANES), f32)
+    ids = ids_ref[...]
+    comb = comb_ref[...]
+    chosen = ids.shape[1]
+    for k in range(chosen):
+        table += jnp.where(lane == ids[:, k : k + 1], comb[:, k : k + 1], 0.0)
+    high = table.astype(bf)
+    me = idx(c, g, s)
+    xg[me, :, :width] = (x_f * inv * gain_ref[...]).astype(bf)
+    xg[me, :, width:] = high
+    dg[me, :, :width] = dout_ref[...]
+    dg[me, :, width:] = (table - high.astype(f32)).astype(bf)
+
+    pl.semaphore_wait(barrier, len(peers))
+
+    arrays = (xg, dg)
+    first, second = (cx, cy), (cy, cx)
+    offs = [0]
+    for k in range(1, G):
+        offs += [k, -k]
+
+    def z_copy(a, gg, up):
+        i = idx(c, gg, s)
+        to = g + 1 if up else g - 1
+        return rc(arrays[a].at[i], arrays[a].at[i], zs_s.at[a, int(up), gg], zs_r.at[a, gg], (c, to, s))
+
+    def p1_copy(a, gg, cc):
+        i = idx(cc, gg, s)
+        return rc(arrays[a].at[i], arrays[a].at[i], p1_s.at[a, gg], p1_r.at[a, gg], (first[a], g, s))
+
+    def p2_copy(a, j, gg, cc):
+        i = idx(cc, gg, s)
+        return rc(arrays[a].at[i], arrays[a].at[i], p2_s.at[a, j, gg], p2_r.at[a, j, gg], (second[a], g, s))
+
+    def side_copy(a, gg, cc, ss):
+        i = idx(cc, gg, ss)
+        return rc(arrays[a].at[i], arrays[a].at[i], sd_s.at[a, cc, gg], sd_r.at[a, cc, gg], (c, g, o))
+
+    def inside(gg):
+        return jnp.logical_and(gg >= 0, gg < G)
+
+    for off in offs:
+        gg = g + off
+
+        @pl.when(inside(gg))
+        def _(gg=gg, off=off):
+            for a in (0, 1):
+                if off != 0:
+                    z_copy(a, gg, off < 0).wait_recv()
+                if off >= 0:
+                    @pl.when(g > 0)
+                    def _():
+                        z_copy(a, gg, False).start()
+                if off <= 0:
+                    @pl.when(g < G - 1)
+                    def _():
+                        z_copy(a, gg, True).start()
+                p1_copy(a, gg, c).start()
+                p2_copy(a, 0, gg, c).start()
+                side_copy(a, gg, c, s).start()
+
+    for load in loads:
+        load.start()
+
+    for off in offs:
+        gg = g + off
+
+        @pl.when(inside(gg))
+        def _(gg=gg):
+            for a in (0, 1):
+                p1_copy(a, gg, first[a]).wait_recv()
+                p2_copy(a, 1, gg, first[a]).start()
+                side_copy(a, gg, first[a], s).start()
+
+    for off in offs:
+        gg = g + off
+
+        @pl.when(inside(gg))
+        def _(gg=gg):
+            for a in (0, 1):
+                p2_copy(a, 0, gg, second[a]).wait_recv()
+                side_copy(a, gg, second[a], s).start()
+            for a in (0, 1):
+                p2_copy(a, 1, gg, cxy).wait_recv()
+                side_copy(a, gg, cxy, s).start()
+
+    for cc in range(4):
+        for gg in range(G):
+            for a in (0, 1):
+                side_copy(a, gg, cc, o).wait_recv()
+    for load in loads:
+        load.wait()
+
+    rows = total // 2
+    mine = (lax.broadcasted_iota(jnp.int32, (rows, LANES), 1) == expert).astype(f32)
+    nt = (((1,), (1,)), ((), ()))
+    tn = (((0,), (0,)), ((), ()))
+    ch = chunks // 2
+
+    def forward(i, gain_sum):
+        b = (i + 1 - y) % 2
+        part = pl.ds(b * ch, ch)
+        at = pl.ds(pl.multiple_of(b * rows, rows), rows)
+        xr = xg[part, :, :width].reshape(rows, width)
+        dr = dg[part, :, :width].reshape(rows, width)
+        weight = xg[part, :, width:].astype(f32).reshape(rows, LANES)
+        weight = weight + dg[part, :, width:].astype(f32).reshape(rows, LANES)
+        weight = jnp.sum(weight * mine, axis=1, keepdims=True)
+        a_gate = jnp.dot(xr, wg[...], preferred_element_type=f32)
+        a_up = jnp.dot(xr, wu[...], preferred_element_type=f32)
+        raw = lax.dot_general(dr, wd[...], nt, preferred_element_type=f32)
+        sig = jax.nn.sigmoid(a_gate)
+        silu = a_gate * sig
+        hidden = silu * a_up
+        dc = jnp.sum(hidden * raw, axis=1, keepdims=True)
+        d_hidden = raw * weight
+        hc = (hidden * weight).astype(bf)
+        d_up = (d_hidden * silu).astype(bf)
+        d_gate = (d_hidden * a_up * sig * (1.0 + a_gate * (1.0 - sig))).astype(bf)
+        act[0, at, :] = d_gate
+        act[1, at, :] = d_up
+        act[2, at, :] = hc
+        dcol = jnp.where(weight > 0.0, dc, 0.0) * mine
+        mo[part, :, width:] = dcol.astype(bf).reshape(ch, count, LANES)
+        out = jnp.dot(hc, wd[...], preferred_element_type=f32)
+        mo[part, :, :width] = out.astype(bf).reshape(ch, count, width)
+        back = lax.dot_general(d_gate, wg[...], nt, preferred_element_type=f32)
+        back += lax.dot_general(d_up, wu[...], nt, preferred_element_type=f32)
+        bo[part, :, :] = back.astype(bf).reshape(ch, count, width)
+        gain_sum = gain_sum + jnp.sum(back * xr.astype(f32), axis=0, keepdims=True)
+
+        for k in range(2):
+            cc = 2 * b + k
+            for gg in range(G):
+                for a in (0, 1):
+                    rs_copy(a, cc, gg, o).start()
+        return gain_sum
+
+    outs = (mo, bo)
+    wide = (full, width)
+
+    def rs_copy(a, cc, gg, ss):
+        return rc(
+            outs[a].at[idx(cc, gg, ss)], rs.at[a, cc * G + gg, :, : wide[a]],
+            rs_s.at[a, cc, gg], rs_r.at[a, cc, gg], (c, g, o),
+        )
+
+    n1, n2 = (cy, cx), (cx, cy)
+
+    def q1_copy(a, j, gg, cc):
+        return rc(
+            outs[a].at[idx(cc, gg, s)], rp1.at[a, j, gg, :, : wide[a]],
+            q1_s.at[a, j, gg], q1_r.at[a, j, gg], (n1[a], g, s),
+        )
+
+    def q2_copy(a, gg, cc):
+        return rc(
+            outs[a].at[idx(cc, gg, s)], rp2.at[a, gg, :, : wide[a]],
+            q2_s.at[a, gg], q2_r.at[a, gg], (n2[a], g, s),
+        )
+
+    def rz_copy(a, up, gg):
+        to = g + 1 if up else g - 1
+        return rc(
+            outs[a].at[idx(c, gg, s)], rz.at[a, int(up), gg, :, : wide[a]],
+            rz_s.at[a, int(up), gg], rz_r.at[a, int(up), gg], (c, to, s),
+        )
+
+    def add(a, cc, gg, terms):
+        i = idx(cc, gg, s)
+        value = outs[a][i].astype(f32)
+        for term in terms:
+            value = value + term[:, : wide[a]].astype(f32)
+        outs[a][i] = value.astype(bf)
+
+    gain_sum = lax.fori_loop(0, 2, forward, jnp.zeros((1, width), f32))
+    dgb[0] = gain_sum / gain_ref[...]
+
+    gain_devs = [(c, g, o), (cx, g, s), (cy, g, s)]
+
+    def dg_copy(k):
+        return rc(dgb.at[k], dgb.at[8 + k], dg_s.at[k], dg_r.at[k], gain_devs[k])
+
+    def dgz_copy(k):
+        return rc(dgb.at[3], dgb.at[8 + 2 + k], dg_s.at[2 + k], dg_r.at[2 + k], (c, (g + k) % G, s))
+
+    dg_copy(0).start()
+
+    order = [(g + G // 2 + i) % G for i in range(G)]
+    for j in (1, 0):
+        for gg in order:
+            for a in (0, 1):
+                cc = cxy if j else n1[a]
+                rs_copy(a, cc, gg, s).wait_recv()
+                add(a, cc, gg, [rs[a, cc * G + gg]])
+                q1_copy(a, j, gg, cc).start()
+
+    dg_copy(0).wait_recv()
+    dgb[1] = dgb[0] + dgb[8]
+    dg_copy(1).start()
+
+    blk = width // 4
+
+    def grads(i, carry):
+        cols = pl.ds(pl.multiple_of(i * blk, blk), blk)
+        xr = xg[:, :, cols].reshape(total, blk)
+        dr = dg[:, :, cols].reshape(total, blk)
+        gwg[cols, :] = lax.dot_general(xr, act[0], tn, preferred_element_type=f32).astype(bf)
+        gwu[cols, :] = lax.dot_general(xr, act[1], tn, preferred_element_type=f32).astype(bf)
+        gwd[:, cols] = lax.dot_general(act[2], dr, tn, preferred_element_type=f32).astype(bf)
+        return carry
+
+    lax.fori_loop(0, 4, grads, 0)
+    stores = [
+        pltpu.make_async_copy(b, a.at[0], o_sem.at[i])
+        for i, (a, b) in enumerate(((gg_hbm, gwg), (gu_hbm, gwu), (gd_hbm, gwd)))
+    ]
+    for store in stores:
+        store.start()
+
+    dg_copy(1).wait_recv()
+    dgb[2] = dgb[1] + dgb[9]
+    dg_copy(2).start()
+
+    for gg in order:
+        for a in (0, 1):
+            rs_copy(a, n2[a], gg, s).wait_recv()
+            q1_copy(a, 1, gg, cxy).wait_recv()
+            add(a, n2[a], gg, [rs[a, n2[a] * G + gg], rp1[a, 1, gg]])
+            q2_copy(a, gg, n2[a]).start()
+
+    dg_copy(2).wait_recv()
+    dgb[3] = dgb[2] + dgb[10]
+    for k in range(1, G):
+        dgz_copy(k).start()
+
+    for gg in order:
+        for a in (0, 1):
+            rs_copy(a, c, gg, s).wait_recv()
+            q1_copy(a, 0, gg, c).wait_recv()
+            q2_copy(a, gg, c).wait_recv()
+            add(a, c, gg, [rs[a, c * G + gg], rp1[a, 0, gg], rp2[a, gg]])
+
+    for k in range(G - 1, 0, -1):
+        for up in (True, False):
+            gg = g + k if up else g - k
+
+            @pl.when(inside(gg))
+            def _(gg=gg, up=up):
+                for a in (0, 1):
+                    @pl.when(g > 0 if up else g < G - 1)
+                    def _():
+                        rz_copy(a, up, gg).wait_recv()
+                        add(a, c, gg, [rz[a, int(up), gg]])
+
+                    rz_copy(a, up, gg).start()
+
+    for a in (0, 1):
+        acc[a, :, : wide[a]] = outs[a][me].astype(f32)
+        for up in (True, False):
+            @pl.when(g > 0 if up else g < G - 1)
+            def _():
+                rz_copy(a, up, g).wait_recv()
+                acc[a, :, : wide[a]] += rz[a, int(up), g, :, : wide[a]].astype(f32)
+
+    x_f = tok_ref[...].astype(f32)
+    inv = lax.rsqrt(jnp.mean(x_f * x_f, axis=1, keepdims=True) + EPS)
+    mixed_ref[...] = (x_f + acc[0, :, :width]).astype(bf)
+    dcs = acc[0, :, width:]
+    for k in range(chosen):
+        dcomb_ref[:, k : k + 1] = jnp.sum(
+            jnp.where(lane == ids_ref[:, k : k + 1], dcs, 0.0), axis=1, keepdims=True
+        )
+    scaled = acc[1, :, :width] * gain_ref[...]
+    dtok_ref[...] = (
+        dout_ref[...].astype(f32)
+        + inv * scaled
+        - x_f * inv * inv * inv * jnp.mean(scaled * x_f, axis=1, keepdims=True)
+    ).astype(bf)
+
+    total_gain = dgb[3]
+    for k in range(1, G):
+        dgz_copy(k).wait_recv()
+        total_gain = total_gain + dgb[8 + 2 + k]
+    dgain_ref[...] = total_gain
+
+    for a in (0, 1):
+        for gg in range(G):
+            for up in (True, False):
+                edge = g < G - 1 if up else g > 0
+                way = gg <= g if up else gg >= g
+
+                @pl.when(jnp.logical_and(edge, way))
+                def _():
+                    z_copy(a, gg, up).wait_send()
+
+                @pl.when(gg > g if up else gg < g)
+                def _():
+                    rz_copy(a, up, gg).wait_send()
+
+            p1_copy(a, gg, c).wait_send()
+            p2_copy(a, 0, gg, c).wait_send()
+            p2_copy(a, 1, gg, first[a]).wait_send()
+            q1_copy(a, 0, gg, n1[a]).wait_send()
+            q1_copy(a, 1, gg, cxy).wait_send()
+            q2_copy(a, gg, n2[a]).wait_send()
+            for cc in range(4):
+                side_copy(a, gg, cc, s).wait_send()
+                rs_copy(a, cc, gg, o).wait_send()
+    for k in range(3):
+        dg_copy(k).wait_send()
+    for k in range(1, G):
+        dgz_copy(k).wait_send()
+    for store in stores:
+        store.wait()
+
+
+def fused(tokens, norm_gain, combine, expert_ids, w_gate, w_up, w_down, d_out):
+    count, width = tokens.shape
+    half = w_gate.shape[2]
+    G = lax.axis_size("grp")
+    devices = lax.axis_size("ctx") * G * lax.axis_size("side")
+    total = devices * count
+    full = width + LANES
+    bf, f32 = jnp.bfloat16, jnp.float32
+    vmem = pl.BlockSpec(memory_space=pltpu.VMEM)
+    hbm = pl.BlockSpec(memory_space=pl.ANY)
+    dma = pltpu.SemaphoreType.DMA
+    outs = pl.pallas_call(
+        lambda *refs: kernel(G, *refs),
+        out_shape=(
+            jax.ShapeDtypeStruct(tokens.shape, bf),
+            jax.ShapeDtypeStruct(tokens.shape, bf),
+            jax.ShapeDtypeStruct((1, width), f32),
+            jax.ShapeDtypeStruct(combine.shape, f32),
+            jax.ShapeDtypeStruct(w_gate.shape, bf),
+            jax.ShapeDtypeStruct(w_up.shape, bf),
+            jax.ShapeDtypeStruct(w_down.shape, bf),
+        ),
+        in_specs=[vmem, vmem, vmem, vmem, hbm, hbm, hbm, vmem],
+        out_specs=(vmem, vmem, vmem, vmem, hbm, hbm, hbm),
+        scratch_shapes=[
+            pltpu.VMEM((devices, count, full), bf),
+            pltpu.VMEM((devices, count, full), bf),
+            pltpu.VMEM((width, half), bf),
+            pltpu.VMEM((width, half), bf),
+            pltpu.VMEM((half, width), bf),
+            pltpu.VMEM((8, LANES), f32),
+            pltpu.VMEM((devices, count, full), bf),
+            pltpu.VMEM((devices, count, width), bf),
+            pltpu.VMEM((2, devices // 2, count, full), bf),
+            pltpu.VMEM((2, 2, G, count, full), bf),
+            pltpu.VMEM((2, G, count, full), bf),
+            pltpu.VMEM((2, 2, G, count, full), bf),
+            pltpu.VMEM((16, 1, width), f32),
+            pltpu.VMEM((3, total, half), bf),
+            pltpu.VMEM((width, half), bf),
+            pltpu.VMEM((width, half), bf),
+            pltpu.VMEM((half, width), bf),
+            pltpu.VMEM((2, count, full), f32),
+            dma((2, 2, G)), dma((2, G)),
+            dma((2, G)), dma((2, G)),
+            dma((2, 2, G)), dma((2, 2, G)),
+            dma((2, 4, G)), dma((2, 4, G)),
+            dma((2, 4, G)), dma((2, 4, G)),
+            dma((2, 2, G)), dma((2, 2, G)),
+            dma((2, G)), dma((2, G)),
+            dma((2, 2, G)), dma((2, 2, G)),
+            dma((8,)), dma((8,)),
+            dma((3,)), dma((3,)),
+        ],
+        compiler_params=pltpu.CompilerParams(
+            collective_id=0, has_side_effects=True, vmem_limit_bytes=60 * 2**20
+        ),
+    )(tokens, norm_gain[None], combine, expert_ids, w_gate, w_up, w_down, d_out)
+    mixed, d_tokens, d_gain, d_combine, g_gate, g_up, g_down = outs
+    return mixed, d_tokens, d_gain[0], d_combine, g_gate, g_up, g_down
+
+
 def solution(mesh):
     in_specs = (
         P(("ctx", "grp", "side"), None),
@@ -167,4 +598,5 @@
         P(("ctx", "grp"), None, "side"),
         P(("ctx", "grp"), "side", None),
     )
-    return jax.shard_map(local, mesh=mesh, in_specs=in_specs, out_specs=out_specs, check_vma=False)
+    body = fused if fits(mesh) else local
+    return jax.shard_map(body, mesh=mesh, in_specs=in_specs, out_specs=out_specs, check_vma=False)

time: 223 us -> 88.6 us (0.40)
  waiting for transfers between devices: 97.2 us -> 0 us
  Pallas kernels: 0 us -> 73.3 us
  blocking collectives: 36.9 us -> 0 us
  matrix products: 31.3 us -> 0 us
  starting transfers between devices: 20.6 us -> 0 us
  between operations: 14.5 us -> 0.65 us
  other arithmetic: 11.7 us -> 0 us
  local copies, waits for them, and re-layouts: 9.45 us -> 14.3 us
    all_to_all x4 -> x0, waiting for transfers between devices: 95 us -> none  [the longest x1 26.4 us: local(): lax.all_to_all(send_rows.reshape(experts, slots, width), ('ctx', 'grp'),...]
    pallas_call x0 -> x1, Pallas kernels: none -> 73.3 us  [fused(): pl.pallas_call(lambda *refs: kernel(G, *refs), out_shape=(jax.ShapeDtypeS...]
    psum x1 -> x0, blocking collectives: 36.9 us -> none  [local(): lax.psum(jnp.sum(d_normed * x_float * inv_rms, axis=0), ('ctx', 'grp', 's...]
    dot_general x14 -> x0, matrix products: 31.3 us -> none  [the longest x1 4.81 us: expert_pass(): lax.dot_general(rows, d_up, (((0,), (0,)), ((), ())), preferred_element_t...]
    all_to_all x4 -> x0, starting transfers between devices: 20.3 us -> none  [the longest x1 8.34 us: local(): lax.all_to_all(send_grads.reshape(experts, slots, width), ('ctx', 'grp'),...]
    unnamed x40 -> x13, local copies, waits for them, and re-layouts: 0.24 us -> 14.3 us
    broadcast_in_dim x3 -> x0, other arithmetic: 9.67 us -> none  [the longest x1 3.27 us: local(): own_down.astype(jnp.bfloat16)[None]]
    reshape x8 -> x0, local copies, waits for them, and re-layouts: 8.37 us -> none  [the longest x1 2.34 us: local(): back_out.reshape(experts, slots, width)]
  transfers between devices with their start and end apart: 10 -> 0, of which waited for: 4 -> 0; matrix products, arithmetic and copies ran while one was open for 19% -> 0% of each run, Pallas kernels for 0% -> 0%
where the time goes in v1:
time: 88.6 us; the launch traced here: 88.2 us
  Pallas kernels  73.3 us (83%)
  local copies, waits for them, and re-layouts  14.3 us (16%)
    pallas_call x1, Pallas kernels, fused(): pl.pallas_call(lambda *refs: kernel(G, *refs), out_shape=(jax.ShapeDtypeS...  73.3 us
    unnamed x13, local copies, waits for them, and re-layouts  14.3 us

profile of v1, /device:TPU:0, one launch (start us, length us, event | category | flops | bytes accessed | tf_op | source)
XLA Modules:
  0.0 88.2 jit_solution(2895061570133988656)
XLA Ops:
  0.6 1.4 %copy.15.refs_2_ = f32[16,8]{1,0:T(8,128)} copy(f32[16,8]{0,1:T(8,128)} %param.10) | data formatting | bytes 1024 | tf_op args[2]
  2.0 1.4 %copy.16.refs_3_ = s32[16,8]{1,0:T(8,128)} copy(s32[16,8]{0,1:T(8,128)} %param.11) | data formatting | bytes 1024 | tf_op args[3]
  3.3 73.3 %shard_map.135 = (bf16[16,2048]{1,0:T(8,128)(2,1)}, bf16[16,2048]{1,0:T(8,128)(2,1)}, f32[1,2048]{1,0:T(1,128)}, f32[16,8]{1,0:T(8,128)}, bf16[1,2048,384]{2,1,0...) custom-call(bf16[16,2048]{1,0:T(8,128)(2,1)} %refs_0_.1, f32[1,2048]{1,0:T(1,128)} %bitcast.2, ...), custom_call_target="tpu_custom_call" | custom-call | tf_op jit(solution)/shard_map/pallas_call | solution.py:530
  76.6 1.4 %copy.17 = f32[16,8]{0,1:T(8,128)} copy(f32[16,8]{1,0:T(8,128)} %get-tuple-element.24) | data formatting | bytes 1024
  78.0 1.5 %copy.24 = bf16[16,2048]{1,0:T(8,128)(2,1)} copy(bf16[16,2048]{1,0:T(8,128)(2,1)} %get-tuple-element.35) | data formatting | bytes 131072
  79.4 1.5 %copy.25 = bf16[16,2048]{1,0:T(8,128)(2,1)} copy(bf16[16,2048]{1,0:T(8,128)(2,1)} %get-tuple-element.36) | data formatting | bytes 131072
  80.9 1.3 %copy.26 = f32[2048]{0:T(1024)} copy(f32[2048]{0:T(1024)} %bitcast.3) | data formatting | bytes 16384
  82.2 0.0 copy-start.1
  82.2 2.8 %copy.27 = bf16[1,2048,384]{2,1,0:T(8,128)(2,1)} copy(bf16[1,2048,384]{2,1,0:T(8,128)(2,1)} %get-tuple-element.39) | data formatting | bytes 3145728
  85.0 0.0 copy-done.1
  85.0 0.0 copy-start
  85.0 1.1 %copy.28 = bf16[1,2048,384]{2,1,0:T(8,128)(2,1)} copy(bf16[1,2048,384]{2,1,0:T(8,128)(2,1)S(1)} %copy-done.1) | data formatting | bytes 3145728
  86.2 0.8 copy-done
  87.0 1.1 %copy.29 = bf16[1,384,2048]{2,1,0:T(8,128)(2,1)} copy(bf16[1,384,2048]{2,1,0:T(8,128)(2,1)S(1)} %copy-done) | data formatting | bytes 3145728
Async XLA Ops:
  82.2 2.8 %copy-start.1 = (bf16[1,2048,384]{2,1,0:T(8,128)(2,1)S(1)}, bf16[1,2048,384]{2,1,0:T(8,128)(2,1)}, u32[]{:S(2)}) copy-start(bf16[1,2048,384]{2,1,0:T(8,128)(2,1)} %get-tuple-element.40) | copy-start | bytes 4718596
  85.0 2.0 %copy-start = (bf16[1,384,2048]{2,1,0:T(8,128)(2,1)S(1)}, bf16[1,384,2048]{2,1,0:T(8,128)(2,1)}, u32[]{:S(2)}) copy-start(bf16[1,384,2048]{2,1,0:T(8,128)(2,1)} %get-tuple-element.41) | copy-start | bytes 4718596

commit v2 on v1

--- a/solution.py
+++ b/solution.py
@@ -160,10 +160,10 @@
 def kernel(
     n_grp,
     tok_ref, gain_ref, comb_ref, ids_ref, wg_hbm, wu_hbm, wd_hbm, dout_ref,
-    mixed_ref, dtok_ref, dgain_ref, dcomb_ref, gg_hbm, gu_hbm, gd_hbm,
-    xg, dg, wg, wu, wd, cw, mo, bo, rs, rp1, rp2, rz, dgb, act, gwg, gwu, gwd, acc,
+    acc, dgain_ref, gwg, gwu, gwd,
+    xg, dg, xs, ds, wg, wu, wd, cw, iw, mo, bo, rs, rp1, rp2, rz, dgb, act,
     zs_s, zs_r, p1_s, p1_r, p2_s, p2_r, sd_s, sd_r,
-    rs_s, rs_r, q1_s, q1_r, q2_s, q2_r, rz_s, rz_r, dg_s, dg_r, w_sem, o_sem,
+    rs_s, rs_r, q1_s, q1_r, q2_s, q2_r, rz_s, rz_r, dg_s, dg_r, w_sem,
 ):
     G = n_grp
     count, width = tok_ref.shape
@@ -198,13 +198,16 @@
 
     x_f = tok_ref[...].astype(f32)
     inv = lax.rsqrt(jnp.mean(x_f * x_f, axis=1, keepdims=True) + EPS)
-    lane = lax.broadcasted_iota(jnp.int32, (count, LANES), 1)
-    table = jnp.zeros((count, LANES), f32)
-    ids = ids_ref[...]
-    comb = comb_ref[...]
-    chosen = ids.shape[1]
+    table = jnp.zeros((LANES, LANES), f32)
+    chosen = ids_ref.shape[0]
+    cw[...] = jnp.zeros_like(cw)
+    iw[...] = jnp.zeros_like(iw)
+    cw[:, :count] = comb_ref[...]
+    iw[:, :count] = ids_ref[...]
+    row = lax.broadcasted_iota(jnp.int32, (LANES, LANES), 0)
     for k in range(chosen):
-        table += jnp.where(lane == ids[:, k : k + 1], comb[:, k : k + 1], 0.0)
+        table += jnp.where(row == iw[k : k + 1, :], cw[k : k + 1, :], 0.0)
+    table = table.T[:count]
     high = table.astype(bf)
     me = idx(c, g, s)
     xg[me, :, :width] = (x_f * inv * gain_ref[...]).astype(bf)
@@ -216,9 +219,14 @@
 
     arrays = (xg, dg)
     first, second = (cx, cy), (cy, cx)
-    offs = [0]
-    for k in range(1, G):
-        offs += [k, -k]
+    upper = (2 * g) // G
+
+    def place(i):
+        return (1 - upper) * (G - 1 - i) + upper * i
+
+    own = place(g)
+    far = [place(i + jnp.where(own <= i, 1, 0)) for i in range(G - 1)] + [g]
+    near = far[::-1]
 
     def z_copy(a, gg, up):
         i = idx(c, gg, s)
@@ -237,53 +245,47 @@
         i = idx(cc, gg, ss)
         return rc(arrays[a].at[i], arrays[a].at[i], sd_s.at[a, cc, gg], sd_r.at[a, cc, gg], (c, g, o))
 
-    def inside(gg):
-        return jnp.logical_and(gg >= 0, gg < G)
-
-    for off in offs:
-        gg = g + off
-
-        @pl.when(inside(gg))
-        def _(gg=gg, off=off):
-            for a in (0, 1):
-                if off != 0:
-                    z_copy(a, gg, off < 0).wait_recv()
-                if off >= 0:
-                    @pl.when(g > 0)
-                    def _():
-                        z_copy(a, gg, False).start()
-                if off <= 0:
-                    @pl.when(g < G - 1)
-                    def _():
-                        z_copy(a, gg, True).start()
-                p1_copy(a, gg, c).start()
-                p2_copy(a, 0, gg, c).start()
-                side_copy(a, gg, c, s).start()
-
-    for load in loads:
-        load.start()
-
-    for off in offs:
-        gg = g + off
-
-        @pl.when(inside(gg))
-        def _(gg=gg):
-            for a in (0, 1):
-                p1_copy(a, gg, first[a]).wait_recv()
-                p2_copy(a, 1, gg, first[a]).start()
-                side_copy(a, gg, first[a], s).start()
-
-    for off in offs:
-        gg = g + off
-
-        @pl.when(inside(gg))
-        def _(gg=gg):
-            for a in (0, 1):
-                p2_copy(a, 0, gg, second[a]).wait_recv()
-                side_copy(a, gg, second[a], s).start()
-            for a in (0, 1):
-                p2_copy(a, 1, gg, cxy).wait_recv()
-                side_copy(a, gg, cxy, s).start()
+    def along_z(gg, first_step):
+        for a in (0, 1):
+            if not first_step:
+                z_copy(a, gg, True).wait_recv()
+
+            @pl.when(jnp.logical_and(gg >= g, g > 0))
+            def _():
+                z_copy(a, gg, False).start()
+
+            @pl.when(jnp.logical_and(gg <= g, g < G - 1))
+            def _():
+                z_copy(a, gg, True).start()
+
+            p1_copy(a, gg, c).start()
+            p2_copy(a, 0, gg, c).start()
+            side_copy(a, gg, c, s).start()
+
+    def along_first(gg):
+        for a in (0, 1):
+            p1_copy(a, gg, first[a]).wait_recv()
+            p2_copy(a, 1, gg, first[a]).start()
+            side_copy(a, gg, first[a], s).start()
+
+    def along_second(gg):
+        for a in (0, 1):
+            p2_copy(a, 0, gg, second[a]).wait_recv()
+            side_copy(a, gg, second[a], s).start()
+        for a in (0, 1):
+            p2_copy(a, 1, gg, cxy).wait_recv()
+            side_copy(a, gg, cxy, s).start()
+
+    for t in range(G + 2):
+        if t < G:
+            along_z(near[t], t == 0)
+        if t == 0:
+            for load in loads:
+                load.start()
+        if 1 <= t <= G:
+            along_first(near[t - 1])
+        if t >= 2:
+            along_second(near[t - 2])
 
     for cc in range(4):
         for gg in range(G):
@@ -292,20 +294,33 @@
     for load in loads:
         load.wait()
 
-    rows = total // 2
+    per = 2 if G % 2 == 0 else 1
+    rows = 8 * per * count
+    ch = 8 * per
     mine = (lax.broadcasted_iota(jnp.int32, (rows, LANES), 1) == expert).astype(f32)
     nt = (((1,), (1,)), ((), ()))
     tn = (((0,), (0,)), ((), ()))
-    ch = chunks // 2
 
     def forward(i, gain_sum):
-        b = (i + 1 - y) % 2
-        part = pl.ds(b * ch, ch)
-        at = pl.ds(pl.multiple_of(b * rows, rows), rows)
-        xr = xg[part, :, :width].reshape(rows, width)
-        dr = dg[part, :, :width].reshape(rows, width)
-        weight = xg[part, :, width:].astype(f32).reshape(rows, LANES)
-        weight = weight + dg[part, :, width:].astype(f32).reshape(rows, LANES)
+        places = far[i * per : (i + 1) * per]
+        pairs = [(cc, gg) for gg in places for cc in range(4)]
+
+        def fetch(ref, cols):
+            parts = [ref[pl.ds(idx(cc, gg, 0), 2), :, cols].reshape(2 * count, -1) for cc, gg in pairs]
+            return jnp.concatenate(parts, axis=0)
+
+        def put(ref, cols, value):
+            for n, (cc, gg) in enumerate(pairs):
+                part = value[n * 2 * count : (n + 1) * 2 * count]
+                ref[pl.ds(idx(cc, gg, 0), 2), :, cols] = part.reshape(2, count, -1)
+
+        main, rest = slice(0, width), slice(width, full)
+        at = pl.ds(i * rows, rows)
+        xr = fetch(xg, main)
+        dr = fetch(dg, main)
+        xs[at, :] = xr
+        ds[at, :] = dr
+        weight = fetch(xg, rest).astype(f32) + fetch(dg, rest).astype(f32)
         weight = jnp.sum(weight * mine, axis=1, keepdims=True)
         a_gate = jnp.dot(xr, wg[...], preferred_element_type=f32)
         a_up = jnp.dot(xr, wu[...], preferred_element_type=f32)
@@ -322,20 +337,17 @@
         act[1, at, :] = d_up
         act[2, at, :] = hc
         dcol = jnp.where(weight > 0.0, dc, 0.0) * mine
-        mo[part, :, width:] = dcol.astype(bf).reshape(ch, count, LANES)
+        put(mo, rest, dcol.astype(bf))
         out = jnp.dot(hc, wd[...], preferred_element_type=f32)
-        mo[part, :, :width] = out.astype(bf).reshape(ch, count, width)
+        put(mo, main, out.astype(bf))
+        for n, (cc, gg) in enumerate(pairs):
+            rs_copy(0, cc, gg, o).start()
         back = lax.dot_general(d_gate, wg[...], nt, preferred_element_type=f32)
         back += lax.dot_general(d_up, wu[...], nt, preferred_element_type=f32)
-        bo[part, :, :] = back.astype(bf).reshape(ch, count, width)
-        gain_sum = gain_sum + jnp.sum(back * xr.astype(f32), axis=0, keepdims=True)
-
-        for k in range(2):
-            cc = 2 * b + k
-            for gg in range(G):
-                for a in (0, 1):
-                    rs_copy(a, cc, gg, o).start()
-        return gain_sum
+        put(bo, main, back.astype(bf))
+        for n, (cc, gg) in enumerate(pairs):
+            rs_copy(1, cc, gg, o).start()
+        return gain_sum + jnp.sum(back * xr.astype(f32), axis=0, keepdims=True)
 
     outs = (mo, bo)
     wide = (full, width)
@@ -374,7 +386,9 @@
             value = value + term[:, : wide[a]].astype(f32)
         outs[a][i] = value.astype(bf)
 
-    gain_sum = lax.fori_loop(0, 2, forward, jnp.zeros((1, width), f32))
+    gain_sum = jnp.zeros((1, width), f32)
+    for i in range(G // per):
+        gain_sum = forward(i, gain_sum)
     dgb[0] = gain_sum / gain_ref[...]
 
     gain_devs = [(c, g, o), (cx, g, s), (cy, g, s)]
@@ -387,74 +401,74 @@
 
     dg_copy(0).start()
 
-    order = [(g + G // 2 + i) % G for i in range(G)]
-    for j in (1, 0):
-        for gg in order:
+    def back_first(gg):
+        for j, pick in ((1, (cxy, cxy)), (0, n1)):
             for a in (0, 1):
-                cc = cxy if j else n1[a]
+                cc = pick[a]
                 rs_copy(a, cc, gg, s).wait_recv()
                 add(a, cc, gg, [rs[a, cc * G + gg]])
                 q1_copy(a, j, gg, cc).start()
 
-    dg_copy(0).wait_recv()
-    dgb[1] = dgb[0] + dgb[8]
-    dg_copy(1).start()
-
-    blk = width // 4
-
-    def grads(i, carry):
-        cols = pl.ds(pl.multiple_of(i * blk, blk), blk)
-        xr = xg[:, :, cols].reshape(total, blk)
-        dr = dg[:, :, cols].reshape(total, blk)
-        gwg[cols, :] = lax.dot_general(xr, act[0], tn, preferred_element_type=f32).astype(bf)
-        gwu[cols, :] = lax.dot_general(xr, act[1], tn, preferred_element_type=f32).astype(bf)
-        gwd[:, cols] = lax.dot_general(act[2], dr, tn, preferred_element_type=f32).astype(bf)
-        return carry
-
-    lax.fori_loop(0, 4, grads, 0)
-    stores = [
-        pltpu.make_async_copy(b, a.at[0], o_sem.at[i])
-        for i, (a, b) in enumerate(((gg_hbm, gwg), (gu_hbm, gwu), (gd_hbm, gwd)))
-    ]
-    for store in stores:
-        store.start()
-
-    dg_copy(1).wait_recv()
-    dgb[2] = dgb[1] + dgb[9]
-    dg_copy(2).start()
-
-    for gg in order:
+    def back_second(gg):
         for a in (0, 1):
             rs_copy(a, n2[a], gg, s).wait_recv()
             q1_copy(a, 1, gg, cxy).wait_recv()
             add(a, n2[a], gg, [rs[a, n2[a] * G + gg], rp1[a, 1, gg]])
             q2_copy(a, gg, n2[a]).start()
 
-    dg_copy(2).wait_recv()
-    dgb[3] = dgb[2] + dgb[10]
-    for k in range(1, G):
-        dgz_copy(k).start()
-
-    for gg in order:
+    def back_z(gg):
         for a in (0, 1):
             rs_copy(a, c, gg, s).wait_recv()
             q1_copy(a, 0, gg, c).wait_recv()
             q2_copy(a, gg, c).wait_recv()
             add(a, c, gg, [rs[a, c * G + gg], rp1[a, 0, gg], rp2[a, gg]])
-
-    for k in range(G - 1, 0, -1):
-        for up in (True, False):
-            gg = g + k if up else g - k
-
-            @pl.when(inside(gg))
-            def _(gg=gg, up=up):
-                for a in (0, 1):
+            for up in (True, False):
+                @pl.when(gg > g if up else gg < g)
+                def _():
                     @pl.when(g > 0 if up else g < G - 1)
                     def _():
                         rz_copy(a, up, gg).wait_recv()
                         add(a, c, gg, [rz[a, int(up), gg]])
 
                     rz_copy(a, up, gg).start()
+
+    blocks = 8
+    blk = width // blocks
+
+    def grads(i):
+        cols = slice(i * blk, (i + 1) * blk)
+        xr = xs[:, cols]
+        dr = ds[:, cols]
+        gwg[0, cols, :] = lax.dot_general(xr, act[0], tn, preferred_element_type=f32).astype(bf)
+        gwu[0, cols, :] = lax.dot_general(xr, act[1], tn, preferred_element_type=f32).astype(bf)
+        gwd[0, :, cols] = lax.dot_general(act[2], dr, tn, preferred_element_type=f32).astype(bf)
+
+    todo = list(range(blocks))
+    for t in range(G + 3):
+        if t < G:
+            back_first(far[t])
+        if t == 1:
+            dg_copy(0).wait_recv()
+            dgb[1] = dgb[0] + dgb[8]
+            dg_copy(1).start()
+        if t == 3:
+            dg_copy(1).wait_recv()
+            dgb[2] = dgb[1] + dgb[9]
+            dg_copy(2).start()
+        if t == 5:
+            dg_copy(2).wait_recv()
+            dgb[3] = dgb[2] + dgb[10]
+            for k in range(1, G):
+                dgz_copy(k).start()
+        if 2 <= t < G + 2:
+            back_second(far[t - 2])
+        if t >= 3:
+            back_z(far[t - 3])
+        for _ in range(2 if t in (1, G - 1, G) else 1):
+            if todo and t >= 1:
+                grads(todo.pop(0))
+    for i in todo:
+        grads(i)
 
     for a in (0, 1):
         acc[a, :, : wide[a]] = outs[a][me].astype(f32)
@@ -463,21 +477,7 @@
             def _():
                 rz_copy(a, up, g).wait_recv()
                 acc[a, :, : wide[a]] += rz[a, int(up), g, :, : wide[a]].astype(f32)
-
-    x_f = tok_ref[...].astype(f32)
-    inv = lax.rsqrt(jnp.mean(x_f * x_f, axis=1, keepdims=True) + EPS)
-    mixed_ref[...] = (x_f + acc[0, :, :width]).astype(bf)
-    dcs = acc[0, :, width:]
-    for k in range(chosen):
-        dcomb_ref[:, k : k + 1] = jnp.sum(
-            jnp.where(lane == ids_ref[:, k : k + 1], dcs, 0.0), axis=1, keepdims=True
-        )
-    scaled = acc[1, :, :width] * gain_ref[...]
-    dtok_ref[...] = (
-        dout_ref[...].astype(f32)
-        + inv * scaled
-        - x_f * inv * inv * inv * jnp.mean(scaled * x_f, axis=1, keepdims=True)
-    ).astype(bf)
+    acc[1, :, width:] = jnp.zeros((count, LANES), f32)
 
     total_gain = dgb[3]
     for k in range(1, G):
@@ -512,6 +512,37 @@
         dg_copy(k).wait_send()
     for k in range(1, G):
         dgz_copy(k).wait_send()
+
+
+def finish(
+    acc, gain_sum, gwg, gwu, gwd, tok_ref, gain_ref, ids_ref, dout_ref,
+    mixed_ref, dtok_ref, dgain_ref, dcomb_ref, gg_hbm, gu_hbm, gd_hbm, iw, sem,
+):
+    stores = [
+        pltpu.make_async_copy(b, a, sem.at[i])
+        for i, (a, b) in enumerate(((gg_hbm, gwg), (gu_hbm, gwu), (gd_hbm, gwd)))
+    ]
+    for store in stores:
+        store.start()
+    bf, f32 = jnp.bfloat16, jnp.float32
+    count, width = tok_ref.shape
+    x_f = tok_ref[...].astype(f32)
+    inv = lax.rsqrt(jnp.mean(x_f * x_f, axis=1, keepdims=True) + EPS)
+    mixed_ref[...] = (x_f + acc[0, :, :width]).astype(bf)
+    iw[...] = jnp.zeros_like(iw)
+    iw[:, :count] = ids_ref[...]
+    row = lax.broadcasted_iota(jnp.int32, (LANES, LANES), 0)
+    dcs = jnp.concatenate([acc[0, :, width:], jnp.zeros((LANES - count, LANES), f32)], axis=0).T
+    for k in range(ids_ref.shape[0]):
+        got = jnp.sum(jnp.where(row == iw[k : k + 1, :], dcs, 0.0), axis=0, keepdims=True)
+        dcomb_ref[k : k + 1, :] = got[:, :count]
+    scaled = acc[1, :, :width] * gain_ref[...]
+    dtok_ref[...] = (
+        dout_ref[...].astype(f32)
+        + inv * scaled
+        - x_f * inv * inv * inv * jnp.mean(scaled * x_f, axis=1, keepdims=True)
+    ).astype(bf)
+    dgain_ref[...] = gain_sum[...]
     for store in stores:
         store.wait()
 
@@ -527,26 +558,30 @@
     vmem = pl.BlockSpec(memory_space=pltpu.VMEM)
     hbm = pl.BlockSpec(memory_space=pl.ANY)
     dma = pltpu.SemaphoreType.DMA
-    outs = pl.pallas_call(
+    gain = norm_gain[None]
+    combine_t, ids_t = combine.T, expert_ids.T
+    ids_pad = (combine.shape[1], LANES)
+    acc, gain_sum, g_gate, g_up, g_down = pl.pallas_call(
         lambda *refs: kernel(G, *refs),
         out_shape=(
-            jax.ShapeDtypeStruct(tokens.shape, bf),
-            jax.ShapeDtypeStruct(tokens.shape, bf),
+            jax.ShapeDtypeStruct((2, count, full), f32),
             jax.ShapeDtypeStruct((1, width), f32),
-            jax.ShapeDtypeStruct(combine.shape, f32),
             jax.ShapeDtypeStruct(w_gate.shape, bf),
             jax.ShapeDtypeStruct(w_up.shape, bf),
             jax.ShapeDtypeStruct(w_down.shape, bf),
         ),
         in_specs=[vmem, vmem, vmem, vmem, hbm, hbm, hbm, vmem],
-        out_specs=(vmem, vmem, vmem, vmem, hbm, hbm, hbm),
+        out_specs=(vmem,) * 5,
         scratch_shapes=[
             pltpu.VMEM((devices, count, full), bf),
             pltpu.VMEM((devices, count, full), bf),
+            pltpu.VMEM((total, width), bf),
+            pltpu.VMEM((total, width), bf),
             pltpu.VMEM((width, half), bf),
             pltpu.VMEM((width, half), bf),
             pltpu.VMEM((half, width), bf),
-            pltpu.VMEM((8, LANES), f32),
+            pltpu.VMEM(ids_pad, f32),
+            pltpu.VMEM(ids_pad, jnp.int32),
             pltpu.VMEM((devices, count, full), bf),
             pltpu.VMEM((devices, count, width), bf),
             pltpu.VMEM((2, devices // 2, count, full), bf),
@@ -555,10 +590,6 @@
             pltpu.VMEM((2, 2, G, count, full), bf),
             pltpu.VMEM((16, 1, width), f32),
             pltpu.VMEM((3, total, half), bf),
-            pltpu.VMEM((width, half), bf),
-            pltpu.VMEM((width, half), bf),
-            pltpu.VMEM((half, width), bf),
-            pltpu.VMEM((2, count, full), f32),
             dma((2, 2, G)), dma((2, G)),
             dma((2, G)), dma((2, G)),
             dma((2, 2, G)), dma((2, 2, G)),
@@ -568,14 +599,29 @@
             dma((2, G)), dma((2, G)),
             dma((2, 2, G)), dma((2, 2, G)),
             dma((8,)), dma((8,)),
-            dma((3,)), dma((3,)),
+            dma((3,)),
         ],
         compiler_params=pltpu.CompilerParams(
-            collective_id=0, has_side_effects=True, vmem_limit_bytes=60 * 2**20
+            collective_id=0, has_side_effects=True, vmem_limit_bytes=46 * 2**20
         ),
-    )(tokens, norm_gain[None], combine, expert_ids, w_gate, w_up, w_down, d_out)
-    mixed, d_tokens, d_gain, d_combine, g_gate, g_up, g_down = outs
-    return mixed, d_tokens, d_gain[0], d_combine, g_gate, g_up, g_down
+    )(tokens, gain, combine_t, ids_t, w_gate, w_up, w_down, d_out)
+    mixed, d_tokens, d_gain, d_combine, g_gate, g_up, g_down = pl.pallas_call(
+        finish,
+        out_shape=(
+            jax.ShapeDtypeStruct(tokens.shape, bf),
+            jax.ShapeDtypeStruct(tokens.shape, bf),
+            jax.ShapeDtypeStruct((1, width), f32),
+            jax.ShapeDtypeStruct(combine_t.shape, f32),
+            jax.ShapeDtypeStruct(w_gate.shape, bf),
+            jax.ShapeDtypeStruct(w_up.shape, bf),
+            jax.ShapeDtypeStruct(w_down.shape, bf),
+        ),
+        in_specs=[vmem] * 9,
+        out_specs=(vmem,) * 4 + (hbm,) * 3,
+        scratch_shapes=[pltpu.VMEM(ids_pad, jnp.int32), dma((3,))],
+        compiler_params=pltpu.CompilerParams(vmem_limit_bytes=12 * 2**20),
+    )(acc, gain_sum, g_gate, g_up, g_down, tokens, gain, ids_t, d_out)
+    return mixed, d_tokens, d_gain[0], d_combine.T, g_gate, g_up, g_down
 
 
 def solution(mesh):

time: 88.6 us -> 76.6 us (0.86)
  local copies, waits for them, and re-layouts: 14.3 us -> 6.56 us
  Pallas kernels: 73.3 us -> 69 us
    unnamed x13 -> x14, local copies, waits for them, and re-layouts: 14.3 us -> 6.56 us
    pallas_call x1, Pallas kernels: 73.3 us -> 66.1 us  [fused(): pl.pallas_call(lambda *refs: kernel(G, *refs), out_shape=(jax.ShapeDtypeS...]
    pallas_call x0 -> x1, Pallas kernels: none -> 2.88 us  [fused(): pl.pallas_call(finish, out_shape=(jax.ShapeDtypeStruct(tokens.shape, bf),...]
where the time goes in v2:
time: 76.6 us; the launch traced here: 76.2 us
  Pallas kernels  69 us (90%)
  local copies, waits for them, and re-layouts  6.56 us (9%)
    pallas_call x1, Pallas kernels, fused(): pl.pallas_call(lambda *refs: kernel(G, *refs), out_shape=(jax.ShapeDtypeS...  66.1 us
    unnamed x14, local copies, waits for them, and re-layouts  6.56 us
    pallas_call x1, Pallas kernels, fused(): pl.pallas_call(finish, out_shape=(jax.ShapeDtypeStruct(tokens.shape, bf),...  2.88 us

profile of v2, /device:TPU:0, one launch (start us, length us, event | category | flops | bytes accessed | tf_op | source)
XLA Modules:
  0.0 76.2 jit_solution(14526376821205790397)
XLA Ops:
  0.6 0.0 copy-start
  0.6 1.4 %copy-done = bf16[1,2048,384]{2,1,0:T(8,128)(2,1)S(1)} copy-done((bf16[1,2048,384]{2,1,0:T(8,128)(2,1)S(1)}, bf16[1,2048,384]{2,1,0:T(8,128)(2,1)}, u32[]{:S(2)}) %copy-start) | copy-done | bytes 1572888
  2.0 0.0 copy-start.1
  2.0 1.4 %copy-done.1 = bf16[1,2048,384]{2,1,0:T(8,128)(2,1)S(1)} copy-done((bf16[1,2048,384]{2,1,0:T(8,128)(2,1)S(1)}, bf16[1,2048,384]{2,1,0:T(8,128)(2,1)}, u32[]{:S(2)}) %copy-start.1) | copy-done | bytes 1572888
  3.5 0.0 copy-start.2
  3.5 0.8 %copy-done.2 = bf16[16,2048]{1,0:T(8,128)(2,1)S(1)} copy-done((bf16[16,2048]{1,0:T(8,128)(2,1)S(1)}, bf16[16,2048]{1,0:T(8,128)(2,1)}, u32[]{:S(2)}) %copy-start.2) | copy-done | bytes 65560
  4.3 0.0 copy-start.3
  4.3 0.8 %copy-done.3 = bf16[16,2048]{1,0:T(8,128)(2,1)S(1)} copy-done((bf16[16,2048]{1,0:T(8,128)(2,1)S(1)}, bf16[16,2048]{1,0:T(8,128)(2,1)}, u32[]{:S(2)}) %copy-start.3) | copy-done | bytes 65560
  5.1 0.0 copy-start.4
  5.1 0.7 copy-done.4
  5.8 0.0 copy-start.5
  5.8 0.7 copy-done.5
  6.5 0.0 copy-start.6
  6.5 0.7 copy-done.6
  7.2 66.1 %shard_map.135 = (f32[2,16,2176]{2,1,0:T(8,128)S(1)}, f32[1,2048]{1,0:T(1,128)S(1)}, bf16[1,2048,384]{2,1,0:T(8,128)(2,1)S(1)}, bf16[1,2048,384]{2,1,0:T(8,128)(2,1)S(1)}, bf16[1,384,2048]{2,1,0:T(8,128)(2,1)S(1)}) custom-call(bf16[16,2048]{1,0:T(8,128)(2,1)S(1)} %copy-done.2, f32[1,2048]{1,0:T(1,128)S(1)} %bitcast.5, f32[8,16]{1,0:T(8,128)S(1)} %bitcast.9, ...), custom_call_target="tpu_custom_call" | custom-call | tf_op jit(solution)/shard_map/pallas_call | solution.py:564
  73.4 2.9 %shard_map.136 = (bf16[16,2048]{1,0:T(8,128)(2,1)}, bf16[16,2048]{1,0:T(8,128)(2,1)}, f32[1,2048]{1,0:T(1,128)}, f32[8,16]{1,0:T(8,128)}, bf16[1,2048,384]{2,1,0...) custom-call(f32[2,16,2176]{2,1,0:T(8,128)S(1)} %get-tuple-element.19.acc, ...), custom_call_target="tpu_custom_call" | custom-call | tf_op jit(solution)/shard_map/pallas_call | solution.py:608
Async XLA Ops:
  0.6 1.4 %copy-start = (bf16[1,2048,384]{2,1,0:T(8,128)(2,1)S(1)}, bf16[1,2048,384]{2,1,0:T(8,128)(2,1)}, u32[]{:S(2)}) copy-start(bf16[1,2048,384]{2,1,0:T(8,128)(2,1)} %refs_4_.1) | copy-start | bytes 4718596
  2.0 1.4 %copy-start.1 = (bf16[1,2048,384]{2,1,0:T(8,128)(2,1)S(1)}, bf16[1,2048,384]{2,1,0:T(8,128)(2,1)}, u32[]{:S(2)}) copy-start(bf16[1,2048,384]{2,1,0:T(8,128)(2,1)} %refs_5_.1) | copy-start | bytes 4718596
  3.5 0.8 %copy-start.2 = (bf16[16,2048]{1,0:T(8,128)(2,1)S(1)}, bf16[16,2048]{1,0:T(8,128)(2,1)}, u32[]{:S(2)}) copy-start(bf16[16,2048]{1,0:T(8,128)(2,1)} %tok_ref.1) | copy-start | bytes 196612
  4.3 0.8 %copy-start.3 = (bf16[16,2048]{1,0:T(8,128)(2,1)S(1)}, bf16[16,2048]{1,0:T(8,128)(2,1)}, u32[]{:S(2)}) copy-start(bf16[16,2048]{1,0:T(8,128)(2,1)} %dout_ref.1) | copy-start | bytes 196612
  5.1 0.7 copy-start.4
  5.8 0.7 copy-start.5
  6.5 0.7 copy-start.6
